TPU v7x, 256 devices: a whole 4x4x8 slice. The times are simulated.
256 devices in a mesh: panel: 32 (over z, y_lo, core), rep: 8 (over x, y_hi).
Axes of the slice: x: 4, y: 4 (y_hi: 2, y_lo: 2; y = y_hi * 2 + y_lo), z: 8, core: 2. Of those that a mesh axis runs over, the one named last changes fastest.
Arguments:
- x_src: bfloat16 [4096, 128], P('panel'), may hold values from -6 to 6
- x_dst: bfloat16 [131072, 128], P(('panel', 'rep')), may hold values from -6 to 6
- weight: bfloat16 [128, 512], replicated, may hold values from -0.5 to 0.5
- att_src: float32 [8, 64], replicated, may hold values from -0.75 to 0.75
- att_dst: float32 [8, 64], replicated, may hold values from -0.75 to 0.75
- grad_out: bfloat16 [131072, 512], P(('panel', 'rep')), may hold values from -6 to 6
- block_rows: int32 [4096], P(('panel', 'rep')), may hold values from 0 to 3, as said below
- block_cols: int32 [4096], P(('panel', 'rep')), may hold values from 0 to 31
- block_masks: int32 [4096, 128, 128], P(('panel', 'rep')), may hold values from 0 to 1, as said below
- block_counts: int32 [256], P(('panel', 'rep')), may hold values from 2 to 16, as said below
Outputs:
- grad_src: float32 [4096, 128], P('panel')
- grad_dst: float32 [131072, 128], P(('panel', 'rep'))
- grad_weight: float32 [128, 512], replicated
- grad_att_src: float32 [8, 64], replicated
- grad_att_dst: float32 [8, 64], replicated
Inputs may be any that keep to these rules, and one draw needn't show every extreme that they name: `block_counts`: live block slots of one device; at least one device has exactly 16. The pairs of block_rows and block_cols within one device's 16 slots are distinct. `block_masks`: slots at or after a device's count of live blocks hold only zeros.
All inputs are finite; a program needn't handle non-finite values.
Results may differ from a plain program's by a relative error of at most 0.012.
The roundings to bfloat16 on the way count: a program that leaves them out, or rounds other values in their place, can miss the bound.
Values may be sent and summed in bfloat16 or wider, within the bound.
No kernel may reach another device: no remote copies, remote signals or barrier semaphores. Data moves between devices by JAX's collectives and lax.ppermute only.
A program may use at most 128 MiB of HBM per device.

v0:
```python
import math
import jax
import jax.numpy as jnp
from jax import lax
from jax.sharding import PartitionSpec as P

HIGHEST_PRECISION = lax.Precision.HIGHEST


def smooth_leaky(values):
    return 0.2 * values + 0.8 * jax.nn.softplus(values)


def smooth_slope(values):
    return 0.2 + 0.8 * jax.nn.sigmoid(values)


def shards(
    x_src,
    x_dst,
    weight,
    att_src,
    att_dst,
    grad_out,
    block_rows,
    block_cols,
    block_masks,
    block_counts,
):
    num_heads, head_dim = att_src.shape
    model_width = weight.shape[1]
    block_size = block_masks.shape[1]
    dest_count = x_dst.shape[0]
    source_local = x_src.shape[0]
    slot_count = block_rows.shape[0]
    proj_own = jnp.dot(x_src, weight, preferred_element_type=jnp.float32).astype(jnp.bfloat16)
    proj_all = lax.all_gather(proj_own, "panel", axis=0, tiled=True)
    source_total = proj_all.shape[0]
    dest_blocks = dest_count // block_size
    source_blocks = source_total // block_size
    source_feats = proj_all.reshape(source_total, num_heads, head_dim)
    score_src = jnp.einsum(
        "jhk,hk->hj", source_feats.astype(jnp.float32), att_src, precision=HIGHEST_PRECISION
    )
    proj_dst = jnp.dot(x_dst, weight, preferred_element_type=jnp.float32).astype(jnp.bfloat16)
    feats = proj_dst.reshape(dest_count, num_heads, head_dim)
    feats_wide = feats.astype(jnp.float32)
    score_d = jnp.einsum("ihk,hk->hi", feats_wide, att_dst, precision=HIGHEST_PRECISION)
    score_own = jnp.einsum("ihk,hk->hi", feats_wide, att_src, precision=HIGHEST_PRECISION)
    cotan = grad_out.reshape(dest_count, num_heads, head_dim)
    cotan_wide = cotan.astype(jnp.float32)
    live_count = block_counts[0]
    score_d_blocks = score_d.reshape(num_heads, dest_blocks, block_size)
    score_src_blocks = score_src.reshape(num_heads, source_blocks, block_size)
    source_row_blocks = source_feats.reshape(source_blocks, block_size, num_heads, head_dim)
    cotan_blocks = cotan.reshape(dest_blocks, block_size, num_heads, head_dim)
    group = math.gcd(slot_count, 16)
    groups = slot_count // group
    alive_all = (jnp.arange(slot_count, dtype=jnp.int32) < live_count).astype(jnp.float32)
    slot_inputs = (
        block_rows.reshape(groups, group),
        block_cols.reshape(groups, group),
        block_masks.reshape(groups, group, block_size, block_size),
        alive_all.reshape(groups, group),
    )

    def group_scores(rows, cols, masks, alive):
        dest_hot = (rows[:, None] == jnp.arange(dest_blocks, dtype=jnp.int32)[None, :]).astype(
            jnp.float32
        )
        source_hot = (cols[:, None] == jnp.arange(source_blocks, dtype=jnp.int32)[None, :]).astype(
            jnp.float32
        )
        score_rows = jnp.einsum(
            "gd,hdu->ghu", dest_hot, score_d_blocks, precision=HIGHEST_PRECISION
        )
        score_cols = jnp.einsum(
            "gs,hsv->ghv", source_hot, score_src_blocks, precision=HIGHEST_PRECISION
        )
        pre_score = score_rows[:, :, :, None] + score_cols[:, :, None, :]
        edge_mask = masks.astype(jnp.float32) * alive[:, None, None]
        edge_weight = jnp.exp(smooth_leaky(pre_score)) * edge_mask[:, None]
        source_rows = jnp.take(source_row_blocks, cols, axis=0)
        return (dest_hot, source_hot, pre_score, edge_weight, source_rows)

    def forward_group(carried_fwd, slot_group):
        denominator, numerator = carried_fwd
        rows, cols, masks, alive = slot_group
        dest_hot, source_hot, pre_score, edge_weight, source_rows = group_scores(
            rows, cols, masks, alive
        )
        part_num = jnp.einsum(
            "ghij,gjhk->gihk",
            edge_weight.astype(jnp.bfloat16),
            source_rows,
            preferred_element_type=jnp.float32,
        )
        denominator = denominator + jnp.einsum(
            "gd,ghi->hdi", dest_hot, edge_weight.sum(axis=3), precision=HIGHEST_PRECISION
        )
        numerator = numerator + jnp.einsum(
            "gd,gihk->dihk", dest_hot, part_num, precision=HIGHEST_PRECISION
        )
        return ((denominator, numerator), None)

    (denominator_blocks, numerator_blocks), _ = lax.scan(
        forward_group,
        (
            jnp.zeros((num_heads, dest_blocks, block_size), jnp.float32),
            jnp.zeros((dest_blocks, block_size, num_heads, head_dim), jnp.float32),
        ),
        slot_inputs,
    )
    denominator = denominator_blocks.reshape(num_heads, dest_count)
    numerator = numerator_blocks.reshape(dest_count, num_heads, head_dim)
    pre_self = score_d + score_own
    self_weight = jnp.exp(smooth_leaky(pre_self))
    denominator = denominator + self_weight
    numerator = numerator + self_weight.T[:, :, None] * feats_wide
    attended = numerator / denominator.T[:, :, None]
    centred = jnp.sum(cotan_wide * attended, axis=2).T
    denominator_full = denominator.reshape(num_heads, dest_blocks, block_size)
    centred_full = centred.reshape(num_heads, dest_blocks, block_size)

    def backward_group(carried_bwd, slot_group):
        grad_source, grad_score_src, grad_score_dst = carried_bwd
        rows, cols, masks, alive = slot_group
        dest_hot, source_hot, pre_score, edge_weight, source_rows = group_scores(
            rows, cols, masks, alive
        )
        denom_rows = jnp.einsum(
            "gd,hdi->ghi", dest_hot, denominator_full, precision=HIGHEST_PRECISION
        )
        attention = edge_weight / denom_rows[:, :, :, None]
        cotan_rows = jnp.take(cotan_blocks, rows, axis=0)
        pair_grad = jnp.einsum(
            "gihk,gjhk->ghij", cotan_rows, source_rows, preferred_element_type=jnp.float32
        )
        centred_rows = jnp.einsum(
            "gd,hdi->ghi", dest_hot, centred_full, precision=HIGHEST_PRECISION
        )
        score_grad = attention * (pair_grad - centred_rows[:, :, :, None]) * smooth_slope(pre_score)
        feat_grad = jnp.einsum(
            "ghij,gihk->gjhk",
            attention.astype(jnp.bfloat16),
            cotan_rows,
            preferred_element_type=jnp.float32,
        )
        grad_source = grad_source + jnp.einsum(
            "gs,gjhk->sjhk", source_hot, feat_grad, precision=HIGHEST_PRECISION
        )
        grad_score_src = grad_score_src + jnp.einsum(
            "gs,ghj->hsj", source_hot, score_grad.sum(axis=2), precision=HIGHEST_PRECISION
        )
        grad_score_dst = grad_score_dst + jnp.einsum(
            "gd,ghi->hdi", dest_hot, score_grad.sum(axis=3), precision=HIGHEST_PRECISION
        )
        return ((grad_source, grad_score_src, grad_score_dst), None)

    (grad_source_blocks, grad_score_src_blocks, grad_score_dst_blocks), _ = lax.scan(
        backward_group,
        (
            jnp.zeros((source_blocks, block_size, num_heads, head_dim), jnp.float32),
            jnp.zeros((num_heads, source_blocks, block_size), jnp.float32),
            jnp.zeros((num_heads, dest_blocks, block_size), jnp.float32),
        ),
        slot_inputs,
    )
    grad_source = grad_source_blocks.reshape(source_total, num_heads, head_dim)
    grad_score_src = grad_score_src_blocks.reshape(num_heads, source_total)
    grad_score_dst = grad_score_dst_blocks.reshape(num_heads, dest_count)
    self_attention = self_weight / denominator
    self_pair = jnp.sum(cotan_wide * feats_wide, axis=2).T
    self_grad = self_attention * (self_pair - centred) * smooth_slope(pre_self)
    grad_score_dst = grad_score_dst + self_grad
    grad_dest = (
        self_attention.T[:, :, None] * cotan_wide
        + self_grad.T[:, :, None] * att_src[None]
        + grad_score_dst.T[:, :, None] * att_dst[None]
    )
    grad_source = grad_source + grad_score_src.T[:, :, None] * att_src[None]
    att_src_part = jnp.einsum(
        "hj,jhk->hk", grad_score_src, source_feats.astype(jnp.float32), precision=HIGHEST_PRECISION
    ) + jnp.einsum("hi,ihk->hk", self_grad, feats_wide, precision=HIGHEST_PRECISION)
    att_dst_part = jnp.einsum("hi,ihk->hk", grad_score_dst, feats_wide, precision=HIGHEST_PRECISION)
    weight_t = weight.astype(jnp.float32).T
    source_flat = grad_source.reshape(source_total, model_width)
    dest_flat = grad_dest.reshape(dest_count, model_width)
    grad_dst = jnp.dot(dest_flat, weight_t, precision=HIGHEST_PRECISION)
    weight_part = jnp.dot(x_dst.astype(jnp.float32).T, dest_flat, precision=HIGHEST_PRECISION)
    share_rows = source_local // lax.axis_size("rep")
    share_start = lax.axis_index("rep") * share_rows
    panel_part = lax.psum_scatter(source_flat, "panel", scatter_dimension=0, tiled=True)
    panel_sum = lax.psum(panel_part, "rep")
    own_share = lax.dynamic_slice_in_dim(panel_sum, share_start, share_rows, 0)
    grad_src = jnp.dot(panel_sum, weight_t, precision=HIGHEST_PRECISION)
    own_inputs = lax.dynamic_slice_in_dim(x_src, share_start, share_rows, 0).astype(jnp.float32)
    weight_part = weight_part + jnp.dot(own_inputs.T, own_share, precision=HIGHEST_PRECISION)
    grad_weight, grad_att_src, grad_att_dst = lax.psum(
        (weight_part, att_src_part, att_dst_part), ("panel", "rep")
    )
    return (grad_src, grad_dst, grad_weight, grad_att_src, grad_att_dst)


def solution(mesh):
    return jax.shard_map(
        shards,
        mesh=mesh,
        in_specs=(
            P("panel", None),
            P(("panel", "rep"), None),
            P(),
            P(),
            P(),
            P(("panel", "rep"), None),
            P(("panel", "rep")),
            P(("panel", "rep")),
            P(("panel", "rep"), None, None),
            P(("panel", "rep")),
        ),
        out_specs=(P("panel", None), P(("panel", "rep"), None), P(), P(), P()),
        check_vma=False,
    )
```

profile of v0, /device:TPU:2, one launch (start us, length us, event | category | flops | bytes accessed | tf_op | source)
XLA Modules:
  0.0 674.6 jit_solution(18316904664663348412)
XLA Ops:
  7.2 0.0 copy-start
  7.2 0.0 copy-start.7
  7.2 0.0 copy-start.6
  7.2 0.0 all-gather.2.cloned.1.call-start
  7.3 0.8 copy-done
  8.1 1.6 convolution_convert_fusion.1
  9.7 0.0 all-gather.2.cloned.1.call-update
  9.7 0.0 reduce-scatter.2.cloned.1.call-start
  9.7 2.1 copy.48
  11.8 1.6 reshape.148
  13.4 1.2 convolution_convert_fusion
  14.7 1.0 fusion.98
  15.7 0.9 fusion.94
  17.3 0.6 copy.39
  17.9 0.8 mul.185
  18.7 0.7 compare_select_fusion.3
  19.4 0.9 gather_fusion
  20.3 0.0 copy-done.9
  20.4 0.3 fusion.100
  20.7 2.4 convert_multiply_fusion.2
  23.1 57.2 %all-gather.2.cloned.1.call-done = bf16[4096,512]{1,0:T(8,128)(2,1)} async-done(((bf16[128,512]{1,0:T(8,128)(2,1)}), bf16[4096,512]{1,0:T(8,128)(2,1)}) %all-gather.2.cloned.1.call-update) | async-done | bytes 4194320 | tf_op jit(solution)/shard_map/all_gather | solution.py:37
  80.3 6.4 copy.41
  86.7 3.9 fusion.99
  90.6 0.1 copy.113
  90.7 0.2 fusion.38
  91.0 9.5 %fusion.23 = f32[16,8,128]{2,1,0:T(8,128)S(1)} fusion(f32[16,128,128]{2,1,0:T(8,128)} %convert_multiply_fusion.2, f32[16,8,128]{2,1,0:T(8,128)S(1)} %copy.42, f32[16,8,128]{2,1,0:T(8,128)S(1)} %copy.40), kind=kLoop, calls=%fused_computation.33 | loop fusion | flops 25149440 | bytes 1245184 | tf_op jit(solution)/shard_map/while/body/eval_jaxpr/reduce_sum | solution.py:99
  100.4 0.1 convolution_bitcast_fusion.2
  100.7 11.2 %reshape.149 = bf16[32,128,8,64]{3,2,1,0:T(8,128)(2,1)} reshape(bf16[4096,512]{1,0:T(8,128)(2,1)} %all-gather.2.cloned.1.call-done) | data formatting | bytes 8388608 | tf_op jit(solution)/shard_map/reshape;reshape | solution.py:55
  111.8 9.1 %copy.47 = bf16[32,128,8,64]{1,3,2,0:T(8,128)(2,1)} copy(bf16[32,128,8,64]{3,2,1,0:T(8,128)(2,1)} %reshape.149) | data formatting | bytes 8388608 | tf_op jit(solution)/shard_map/reshape;reshape | solution.py:55
  120.9 4.3 gather_fusion.1
  125.3 9.9 %fusion.27 = f32[16,128,8,64]{1,3,2,0:T(8,128)S(1)} fusion(f32[16,128,128]{2,1,0:T(8,128)} %convert_multiply_fusion.2, f32[16,8,128]{2,1,0:T(8,128)S(1)} %copy.42, f32[16,8,128]{2,1,0:T(8,128)S(1)} %copy.40, bf16[16,128,8,64]{1,3,2,0:T(8,128)(2,1)} %gather_fusion.1, pred[16]{0:T(512)(128)(4,1)S(1)} %get-tuple-element.104), kind=kOutput, calls=%fused_computation.35 | convolution fusion | flops 294649856 | bytes 7471120 | tf_op jit(solution)/shard_map/while/body/eval_jaxpr/ghij,gjhk->gihk/dot_general | solution.py:92
  135.1 5.0 fusion.14
  140.1 2.6 reshape.108
  142.8 1.6 fusion.33
  144.4 0.2 fusion.89
  144.6 0.2 fusion.91
  144.9 11.8 %fusion.24 = f32[16,128,8,64]{1,3,2,0:T(8,128)S(1)} fusion(f32[16,8,128]{2,1,0:T(8,128)S(1)} %copy.44, f32[16,128,128]{2,1,0:T(8,128)} %convert_multiply_fusion.2, f32[16,8,128]{2,1,0:T(8,128)S(1)} %copy.42, f32[16,8,128]{2,1,0:T(8,128)S(1)} %copy.40, bf16[16,128,8,64]{1,3,2,0:T(8,128)(2,1)S(1)} %gather_fusion, pred[16]{0:T(512)(128)(4,1)S(1)} %get-tuple-element.105), kind=kOutput, calls=%fused_computation.34 | convolution fusion | flops 296747008 | bytes 7536656 | tf_op jit(solution)/shard_map/while/body/eval_jaxpr/ghij,gihk->gjhk/dot_general | solution.py:143
  156.7 15.4 %fusion.96 = (f32[16,8,128]{2,1,0:T(8,128)S(1)}, f32[16,8,128]{2,1,0:T(8,128)S(1)}) fusion(f32[16,8,128]{2,1,0:T(8,128)S(1)} %copy.50, bf16[16,128,8,64]{1,3,2,0:T(8,128)(2,1)S(1)} %copy-done.1, pred[16]{0:T(512)(128)(4,1)S(1)} %get-tuple-element.104, bf16[16,128,8,64]{1,3,2,0:T(8,128)(2,1)S(1)} %gather_fusion, pred[16]{0:T(512)(128)(4,1)S(1)} %get-tuple-element.105, ...), kind=kOutput, calls=%fused_computation.128 | convolution fusion | flops 316637184 | bytes 5636128 | tf_op jit(solution)/shard_map/while/body/eval_jaxpr/gihk,gjhk->ghij/dot_general | solution.py:136
  172.2 0.3 fusion.42
  172.5 0.1 copy.112
  172.6 5.8 fusion.16
  178.4 12.0 %bitcast_add_fusion = f32[4096,512]{0,1:T(8,128)} fusion(f32[64,8,32,128]{3,2,1,0:T(8,128)S(1)} %bitcast.176, f32[512]{0:T(512)S(1)} %mul.185, f32[4096,8]{0,1:T(8,128)S(1)} %bitcast.183), kind=kLoop, calls=%fused_computation.22 | loop fusion | flops 4194304 | bytes 16910336 | tf_op jit(solution)/shard_map/add | solution.py:181
  190.4 0.0 reduce-scatter.2.cloned.1.call-update
  190.5 0.0 all-reduce.4.cloned.1.call-start
  190.5 0.6 copy-done.8
  191.1 0.1 mul.201
  191.2 0.1 convolution_bitcast_fusion.1
  191.4 0.1 copy-done.3
  191.5 0.3 fusion.34
  191.8 0.5 fusion.59
  192.3 0.6 convolution_bitcast_fusion
  192.9 5.1 fusion.103
  198.0 122.5 %reduce-scatter.2.cloned.1.call-done = f32[128,512]{0,1:T(8,128)} async-done(((f32[4096,512]{0,1:T(8,128)}), f32[128,512]{0,1:T(8,128)}) %reduce-scatter.2.cloned.1.call-update) | async-done | bytes 262160 | tf_op jit(solution)/shard_map/reduce_scatter | solution.py:193
  320.5 0.0 all-reduce.4.cloned.1.call-update
  320.5 0.0 all-reduce.6.cloned.1.call-start
  320.5 0.5 fusion.57
  321.0 75.9 %all-reduce = (f32[8,64]{1,0:T(8,128)}, f32[8,64]{1,0:T(8,128)}) all-reduce(f32[8,64]{1,0:T(8,128)S(1)} %add.168, f32[8,64]{1,0:T(8,128)S(1)} %bitcast.197), channel_id=1, replica_groups=mesh['panel'=32,'rep'=8] {'panel','rep'}, use_global_device_ids=true, to_apply=%region_8.10 | all-reduce | flops 1024 | bytes 8192 | tf_op jit(solution)/shard_map/psum | solution.py:199
  396.9 1.7 fusion.102
  398.6 11.2 %all-reduce.4.cloned.1.call-done = f32[128,512]{0,1:T(8,128)} async-done(((f32[128,512]{0,1:T(8,128)}), f32[128,512]{0,1:T(8,128)}) %all-reduce.4.cloned.1.call-update) | async-done | bytes 262160 | tf_op jit(solution)/shard_map/psum | solution.py:194
  409.9 2.0 convolution_add_fusion
  411.9 0.0 all-reduce.6.cloned.1.call-update
  411.9 2.0 fusion.101
  413.8 252.2 %all-reduce.6.cloned.1.call-done = f32[128,512]{0,1:T(8,128)} async-done(((f32[128,512]{0,1:T(8,128)}), f32[128,512]{0,1:T(8,128)}) %all-reduce.6.cloned.1.call-update) | async-done | bytes 262160 | tf_op jit(solution)/shard_map/psum | solution.py:199
  666.1 1.8 copy.54
  (31 shorter events, 0.3 us)
Async XLA Ops:
  7.2 0.9 copy-start
  7.2 13.2 %copy-start.7 = (s32[16]{0:T(128)S(1)}, s32[16]{0:T(128)}, u32[]{:S(2)}) copy-start(s32[16]{0:T(128)} %param.18) | copy-start | bytes 196
  7.2 13.2 %copy-start.6 = (f32[8,64]{1,0:T(8,128)S(1)}, f32[8,64]{1,0:T(8,128)}, u32[]{:S(2)}) copy-start(f32[8,64]{1,0:T(8,128)} %param.15) | copy-start | bytes 6148
  7.2 13.1 %copy-start.9 = (s32[16]{0:T(128)S(1)}, s32[16]{0:T(128)}, u32[]{:S(2)}) copy-start(s32[16]{0:T(128)} %param.19) | copy-start | bytes 196
  7.2 73.1 %all-gather.2.cloned.1.call-start = ((), (), s32[]{:S(2)}) async-start(), calls=%async_computation.1 | async-start | bytes 4325376 | tf_op jit(solution)/shard_map/all_gather | solution.py:37
  9.7 310.8 %reduce-scatter.2.cloned.1.call-start = ((), (), s32[]{:S(2)}) async-start(), calls=%async_computation.2 | async-start | bytes 8650752 | tf_op jit(solution)/shard_map/reduce_scatter | solution.py:193
  125.2 17.5 %copy-start.2 = (bf16[512,512]{0,1:T(8,128)(2,1)S(1)}, bf16[512,512]{0,1:T(8,128)(2,1)}, u32[]{:S(2)}) copy-start(bf16[512,512]{0,1:T(8,128)(2,1)} %copy.48) | copy-start | bytes 1572868
  144.9 11.8 %copy-start.1 = (bf16[16,128,8,64]{1,3,2,0:T(8,128)(2,1)S(1)}, bf16[16,128,8,64]{1,3,2,0:T(8,128)(2,1)}, u32[]{:S(2)}) copy-start(bf16[16,128,8,64]{1,3,2,0:T(8,128)(2,1)} %gather_fusion.1) | copy-start | bytes 6291460
  144.9 11.8 %copy-start.4 = (f32[16,128,128]{2,1,0:T(8,128)S(1)}, f32[16,128,128]{2,1,0:T(8,128)}, u32[]{:S(2)}) copy-start(f32[16,128,128]{2,1,0:T(8,128)} %convert_multiply_fusion.2) | copy-start | bytes 3145732
  190.4 0.7 copy-start.8
  190.4 1.1 copy-start.3
  190.4 1.8 copy-start.5
  190.5 219.4 %all-reduce.4.cloned.1.call-start = ((), (), s32[]{:S(2)}) async-start(), calls=%async_computation.3 | async-start | bytes 524288 | tf_op jit(solution)/shard_map/psum | solution.py:194
  320.5 345.6 %all-reduce.6.cloned.1.call-start = ((), (), s32[]{:S(2)}) async-start(), calls=%async_computation.4 | async-start | bytes 524288 | tf_op jit(solution)/shard_map/psum | solution.py:199
Sparse Core Ops, SparseCore 0:
  10.5 69.7 all-gather.1
  190.6 129.8 reduce-scatter.1
  323.1 86.7 all-reduce.3
  416.6 249.4 all-reduce.5
where the time goes:
time: 682 us; the launch traced here: 675 us
  waiting for transfers between devices  443 us (65%)
  blocking collectives  75.9 us (11%)
  matrix products  70.5 us (10%)
  local copies, waits for them, and re-layouts  43.3 us (6%)
  other arithmetic  26.5 us (4%)
  between operations  15 us (2%)
    psum x1, waiting for transfers between devices, shards(): lax.psum((weight_part, att_src_part, att_dst_part), ('panel', 'rep'))  252 us
    reduce_scatter x1, waiting for transfers between devices, shards(): lax.psum_scatter(source_flat, 'panel', scatter_dimension=0, tiled=True)  122 us
    psum x1, blocking collectives, shards(): lax.psum((weight_part, att_src_part, att_dst_part), ('panel', 'rep'))  75.9 us
    all_gather x1, waiting for transfers between devices, shards(): proj_all = lax.all_gather(proj_own, 'panel', axis=0, tiled=True)  57.2 us
    another operation x2, local copies, waits for them, and re-layouts, shards(): source_feats.reshape(source_blocks, block_size, num_heads, head_dim)  20.2 us
    dot_general x1, matrix products, backward_group(): jnp.einsum('gihk,gjhk->ghij', cotan_rows, source_rows, preferred_element_...  15.4 us
  transfers between devices with their start and end apart: 4, of which 4 were waited for; matrix products, arithmetic and copies ran while one was open for 3% of the time, Pallas kernels for 0%

commit v1 on v0

--- a/solution.py
+++ b/solution.py
@@ -1,10 +1,21 @@
+import functools
 import math
 import jax
 import jax.numpy as jnp
 from jax import lax
 from jax.sharding import PartitionSpec as P
+from jax.lax import psum
 
 HIGHEST_PRECISION = lax.Precision.HIGHEST
+
+
+def make_the_gates(original, group_axis, lane_axis):
+    for m in (group_axis, lane_axis):
+        original = psum(original, m)
+    return original
+
+
+change_indices = functools.partial(make_the_gates, group_axis="rep", lane_axis="panel")
 
 
 def smooth_leaky(values):
@@ -196,8 +207,8 @@
     grad_src = jnp.dot(panel_sum, weight_t, precision=HIGHEST_PRECISION)
     own_inputs = lax.dynamic_slice_in_dim(x_src, share_start, share_rows, 0).astype(jnp.float32)
     weight_part = weight_part + jnp.dot(own_inputs.T, own_share, precision=HIGHEST_PRECISION)
-    grad_weight, grad_att_src, grad_att_dst = lax.psum(
-        (weight_part, att_src_part, att_dst_part), ("panel", "rep")
+    grad_weight, grad_att_src, grad_att_dst = change_indices(
+        (weight_part, att_src_part, att_dst_part)
     )
     return (grad_src, grad_dst, grad_weight, grad_att_src, grad_att_dst)
 

time: 682 us -> 735 us (1.078)
  waiting for transfers between devices: 443 us -> 503 us
    psum x1, waiting for transfers between devices: 11.2 us -> 88.1 us  [shards(): panel_sum = lax.psum(panel_part, 'rep')]
    psum x1 -> x2, waiting for transfers between devices: 252 us -> 233 us  [make_the_gates(): original = psum(original, m)]
    psum x1 -> x2, blocking collectives: 75.9 us -> 74.3 us  [make_the_gates(): original = psum(original, m)]
  transfers between devices with their start and end apart: 4 -> 5, of which waited for: 4 -> 5; matrix products, arithmetic and copies ran while one was open for 3% -> 3% of each run, Pallas kernels for 0% -> 0%
where the time goes in v1:
time: 735 us; the launch traced here: 732 us
  waiting for transfers between devices  503 us (68%)
  blocking collectives  74.3 us (10%)
  matrix products  70.3 us (10%)
  local copies, waits for them, and re-layouts  43.3 us (6%)
  other arithmetic  26.6 us (4%)
  between operations  14.8 us (2%)
    psum x2, waiting for transfers between devices, make_the_gates(): original = psum(original, m)  233 us
    reduce_scatter x1, waiting for transfers between devices, shards(): lax.psum_scatter(source_flat, 'panel', scatter_dimension=0, tiled=True)  124 us
    psum x1, waiting for transfers between devices, shards(): panel_sum = lax.psum(panel_part, 'rep')  88.1 us
    psum x2, blocking collectives, make_the_gates(): original = psum(original, m)  74.3 us
    all_gather x1, waiting for transfers between devices, shards(): proj_all = lax.all_gather(proj_own, 'panel', axis=0, tiled=True)  57.2 us
    another operation x2, local copies, waits for them, and re-layouts, shards(): source_feats.reshape(source_blocks, block_size, num_heads, head_dim)  20.2 us
    dot_general x1, matrix products, backward_group(): jnp.einsum('gihk,gjhk->ghij', cotan_rows, source_rows, preferred_element_...  15.5 us
  transfers between devices with their start and end apart: 5, of which 5 were waited for; matrix products, arithmetic and copies ran while one was open for 3% of the time, Pallas kernels for 0%

profile of v1, /device:TPU:2, one launch (start us, length us, event | category | flops | bytes accessed | tf_op | source)
XLA Modules:
  0.0 732.1 jit_solution(6419881901970289395)
XLA Ops:
  7.2 0.0 copy-start
  7.2 0.0 all-gather.2.cloned.1.call-start
  7.3 0.8 copy-done
  8.1 1.6 convolution_convert_fusion.1
  9.7 0.0 all-gather.2.cloned.1.call-update
  9.7 0.0 reduce-scatter.2.cloned.1.call-start
  9.7 2.1 copy.48
  11.8 1.6 reshape.148
  13.5 1.2 convolution_convert_fusion
  14.7 1.0 fusion.98
  15.7 0.9 fusion.94
  17.3 0.6 copy.39
  17.9 0.8 mul.185
  18.7 0.7 compare_select_fusion.3
  19.4 0.9 gather_fusion
  20.4 0.3 fusion.100
  20.7 2.4 convert_multiply_fusion.2
  23.1 57.2 %all-gather.2.cloned.1.call-done = bf16[4096,512]{1,0:T(8,128)(2,1)} async-done(((bf16[128,512]{1,0:T(8,128)(2,1)}), bf16[4096,512]{1,0:T(8,128)(2,1)}) %all-gather.2.cloned.1.call-update) | async-done | bytes 4194320 | tf_op jit(solution)/shard_map/all_gather | solution.py:48
  80.3 6.4 copy.41
  86.7 3.9 fusion.99
  90.6 0.1 copy.113
  90.7 0.2 fusion.38
  91.0 9.5 %fusion.23 = f32[16,8,128]{2,1,0:T(8,128)S(1)} fusion(f32[16,128,128]{2,1,0:T(8,128)} %convert_multiply_fusion.2, f32[16,8,128]{2,1,0:T(8,128)S(1)} %copy.42, f32[16,8,128]{2,1,0:T(8,128)S(1)} %copy.40), kind=kLoop, calls=%fused_computation.33 | loop fusion | flops 25149440 | bytes 1245184 | tf_op jit(solution)/shard_map/while/body/eval_jaxpr/reduce_sum | solution.py:110
  100.4 0.1 convolution_bitcast_fusion.2
  100.7 11.2 %reshape.149 = bf16[32,128,8,64]{3,2,1,0:T(8,128)(2,1)} reshape(bf16[4096,512]{1,0:T(8,128)(2,1)} %all-gather.2.cloned.1.call-done) | data formatting | bytes 8388608 | tf_op jit(solution)/shard_map/reshape;reshape | solution.py:66
  111.8 9.0 %copy.47 = bf16[32,128,8,64]{1,3,2,0:T(8,128)(2,1)} copy(bf16[32,128,8,64]{3,2,1,0:T(8,128)(2,1)} %reshape.149) | data formatting | bytes 8388608 | tf_op jit(solution)/shard_map/reshape;reshape | solution.py:66
  120.9 4.4 gather_fusion.1
  125.2 9.6 %fusion.27 = f32[16,128,8,64]{1,3,2,0:T(8,128)S(1)} fusion(f32[16,128,128]{2,1,0:T(8,128)} %convert_multiply_fusion.2, f32[16,8,128]{2,1,0:T(8,128)S(1)} %copy.42, f32[16,8,128]{2,1,0:T(8,128)S(1)} %copy.40, bf16[16,128,8,64]{1,3,2,0:T(8,128)(2,1)} %gather_fusion.1, pred[16]{0:T(512)(128)(4,1)S(1)} %get-tuple-element.106), kind=kOutput, calls=%fused_computation.35 | convolution fusion | flops 294649856 | bytes 7471120 | tf_op jit(solution)/shard_map/while/body/eval_jaxpr/ghij,gjhk->gihk/dot_general | solution.py:103
  134.8 5.0 fusion.14
  139.9 2.6 reshape.108
  142.5 1.6 fusion.33
  144.1 0.2 fusion.89
  144.4 0.2 fusion.91
  144.7 11.8 %fusion.24 = f32[16,128,8,64]{1,3,2,0:T(8,128)S(1)} fusion(f32[16,8,128]{2,1,0:T(8,128)S(1)} %copy.44, f32[16,128,128]{2,1,0:T(8,128)} %convert_multiply_fusion.2, f32[16,8,128]{2,1,0:T(8,128)S(1)} %copy.42, f32[16,8,128]{2,1,0:T(8,128)S(1)} %copy.40, bf16[16,128,8,64]{1,3,2,0:T(8,128)(2,1)S(1)} %gather_fusion, pred[16]{0:T(512)(128)(4,1)S(1)} %get-tuple-element.107), kind=kOutput, calls=%fused_computation.34 | convolution fusion | flops 296747008 | bytes 7536656 | tf_op jit(solution)/shard_map/while/body/eval_jaxpr/ghij,gihk->gjhk/dot_general | solution.py:154
  156.5 15.5 %fusion.96 = (f32[16,8,128]{2,1,0:T(8,128)S(1)}, f32[16,8,128]{2,1,0:T(8,128)S(1)}) fusion(f32[16,8,128]{2,1,0:T(8,128)S(1)} %copy.50, bf16[16,128,8,64]{1,3,2,0:T(8,128)(2,1)S(1)} %copy-done.1, pred[16]{0:T(512)(128)(4,1)S(1)} %get-tuple-element.106, bf16[16,128,8,64]{1,3,2,0:T(8,128)(2,1)S(1)} %gather_fusion, pred[16]{0:T(512)(128)(4,1)S(1)} %get-tuple-element.107, ...), kind=kOutput, calls=%fused_computation.128 | convolution fusion | flops 316637184 | bytes 5636128 | tf_op jit(solution)/shard_map/while/body/eval_jaxpr/gihk,gjhk->ghij/dot_general | solution.py:147
  172.0 0.3 fusion.42
  172.3 0.1 copy.112
  172.4 5.8 fusion.16
  178.2 12.1 %bitcast_add_fusion = f32[4096,512]{0,1:T(8,128)} fusion(f32[64,8,32,128]{3,2,1,0:T(8,128)S(1)} %bitcast.176, f32[512]{0:T(512)S(1)} %mul.185, f32[4096,8]{0,1:T(8,128)S(1)} %bitcast.183), kind=kLoop, calls=%fused_computation.22 | loop fusion | flops 4194304 | bytes 16910336 | tf_op jit(solution)/shard_map/add | solution.py:192
  190.3 0.0 reduce-scatter.2.cloned.1.call-update
  190.3 0.0 all-reduce.6.cloned.1.call-start
  190.4 0.6 copy-done.8
  191.0 0.1 mul.201
  191.1 0.1 convolution_bitcast_fusion.1
  191.2 5.1 fusion.103
  196.3 124.2 %reduce-scatter.2.cloned.1.call-done = f32[128,512]{0,1:T(8,128)} async-done(((f32[4096,512]{0,1:T(8,128)}), f32[128,512]{0,1:T(8,128)}) %reduce-scatter.2.cloned.1.call-update) | async-done | bytes 262160 | tf_op jit(solution)/shard_map/reduce_scatter | solution.py:204
  320.5 0.0 all-reduce.6.cloned.1.call-update
  320.5 0.0 all-reduce.8.cloned.1.call-start
  320.6 0.3 fusion.34
  320.9 0.6 convolution_bitcast_fusion
  321.5 88.1 %all-reduce.6.cloned.1.call-done = f32[128,512]{0,1:T(8,128)} async-done(((f32[128,512]{0,1:T(8,128)}), f32[128,512]{0,1:T(8,128)}) %all-reduce.6.cloned.1.call-update) | async-done | bytes 262160 | tf_op jit(solution)/shard_map/psum | solution.py:205
  409.6 2.0 convolution_add_fusion
  411.6 0.0 all-reduce.8.cloned.1.call-update
  411.6 0.0 all-reduce.10.cloned.1.call-start
  411.6 0.5 fusion.59
  412.2 1.7 fusion.102
  413.9 86.2 %all-reduce.8.cloned.1.call-done = f32[128,512]{0,1:T(8,128)} async-done(((f32[128,512]{0,1:T(8,128)}), f32[128,512]{0,1:T(8,128)}) %all-reduce.8.cloned.1.call-update) | async-done | bytes 262160 | tf_op jit(solution)/shard_map/psum | solution.py:14
  500.0 0.0 all-reduce.10.cloned.1.call-update
  500.1 0.5 fusion.57
  500.6 19.7 %all-reduce.1 = (f32[8,64]{1,0:T(8,128)S(1)}, f32[8,64]{1,0:T(8,128)S(1)}) all-reduce(f32[8,64]{1,0:T(8,128)S(1)} %add.174, f32[8,64]{1,0:T(8,128)S(1)} %bitcast.197), channel_id=1, replica_groups=mesh['panel'=32,'rep'=8] {'rep'}, use_global_device_ids=true, to_apply=%region_9.11 | all-reduce | flops 1024 | bytes 8192 | tf_op jit(solution)/shard_map/psum | solution.py:14
  520.3 54.6 %all-reduce = (f32[8,64]{1,0:T(8,128)}, f32[8,64]{1,0:T(8,128)}) all-reduce(f32[8,64]{1,0:T(8,128)S(1)} %get-tuple-element.99, f32[8,64]{1,0:T(8,128)S(1)} %get-tuple-element.100), channel_id=1, replica_groups=mesh['panel'=32,'rep'=8] {'panel'}, use_global_device_ids=true, to_apply=%region_10.12 | all-reduce | flops 1024 | bytes 8192 | tf_op jit(solution)/shard_map/psum | solution.py:14
  574.9 2.0 fusion.101
  576.9 146.9 %all-reduce.10.cloned.1.call-done = f32[128,512]{0,1:T(8,128)} async-done(((f32[128,512]{0,1:T(8,128)}), f32[128,512]{0,1:T(8,128)}) %all-reduce.10.cloned.1.call-update) | async-done | bytes 262160 | tf_op jit(solution)/shard_map/psum | solution.py:14
  723.8 1.8 copy.54
  (35 shorter events, 0.3 us)
Async XLA Ops:
  7.2 0.9 copy-start
  7.2 13.2 %copy-start.7 = (s32[16]{0:T(128)S(1)}, s32[16]{0:T(128)}, u32[]{:S(2)}) copy-start(s32[16]{0:T(128)} %param.18) | copy-start | bytes 196
  7.2 13.2 %copy-start.6 = (f32[8,64]{1,0:T(8,128)S(1)}, f32[8,64]{1,0:T(8,128)}, u32[]{:S(2)}) copy-start(f32[8,64]{1,0:T(8,128)} %param.15) | copy-start | bytes 6148
  7.2 13.1 %copy-start.9 = (s32[16]{0:T(128)S(1)}, s32[16]{0:T(128)}, u32[]{:S(2)}) copy-start(s32[16]{0:T(128)} %param.19) | copy-start | bytes 196
  7.2 73.1 %all-gather.2.cloned.1.call-start = ((), (), s32[]{:S(2)}) async-start(), calls=%async_computation.1 | async-start | bytes 4325376 | tf_op jit(solution)/shard_map/all_gather | solution.py:48
  9.7 310.8 %reduce-scatter.2.cloned.1.call-start = ((), (), s32[]{:S(2)}) async-start(), calls=%async_computation.2 | async-start | bytes 8650752 | tf_op jit(solution)/shard_map/reduce_scatter | solution.py:204
  125.2 17.3 %copy-start.2 = (bf16[512,512]{0,1:T(8,128)(2,1)S(1)}, bf16[512,512]{0,1:T(8,128)(2,1)}, u32[]{:S(2)}) copy-start(bf16[512,512]{0,1:T(8,128)(2,1)} %copy.48) | copy-start | bytes 1572868
  144.6 11.8 %copy-start.1 = (bf16[16,128,8,64]{1,3,2,0:T(8,128)(2,1)S(1)}, bf16[16,128,8,64]{1,3,2,0:T(8,128)(2,1)}, u32[]{:S(2)}) copy-start(bf16[16,128,8,64]{1,3,2,0:T(8,128)(2,1)} %gather_fusion.1) | copy-start | bytes 6291460
  144.7 11.8 %copy-start.4 = (f32[16,128,128]{2,1,0:T(8,128)S(1)}, f32[16,128,128]{2,1,0:T(8,128)}, u32[]{:S(2)}) copy-start(f32[16,128,128]{2,1,0:T(8,128)} %convert_multiply_fusion.2) | copy-start | bytes 3145732
  190.3 0.7 copy-start.8
  190.3 130.3 %copy-start.3 = (bf16[512,512]{0,1:T(8,128)(2,1)S(1)}, bf16[512,512]{0,1:T(8,128)(2,1)}, u32[]{:S(2)}) copy-start(bf16[512,512]{0,1:T(8,128)(2,1)} %copy.48) | copy-start | bytes 1572868
  190.3 130.6 %copy-start.5 = (bf16[512,128]{1,0:T(8,128)(2,1)S(1)}, bf16[512,128]{1,0:T(8,128)(2,1)}, u32[]{:S(2)}) copy-start(bf16[512,128]{1,0:T(8,128)(2,1)} %param.13) | copy-start | bytes 393220
  190.3 219.3 %all-reduce.6.cloned.1.call-start = ((), (), s32[]{:S(2)}) async-start(), calls=%async_computation.3 | async-start | bytes 524288 | tf_op jit(solution)/shard_map/psum | solution.py:205
  320.5 179.5 %all-reduce.8.cloned.1.call-start = ((), (), s32[]{:S(2)}) async-start(), calls=%async_computation.4 | async-start | bytes 524288 | tf_op jit(solution)/shard_map/psum | solution.py:14
  411.6 312.2 %all-reduce.10.cloned.1.call-start = ((), (), s32[]{:S(2)}) async-start(), calls=%async_computation.5 | async-start | bytes 524288 | tf_op jit(solution)/shard_map/psum | solution.py:14
Sparse Core Ops, SparseCore 0:
  10.5 69.7 all-gather.1
  190.4 130.0 reduce-scatter.1
  323.1 86.3 all-reduce.5
  412.8 87.1 all-reduce.7
  502.5 221.2 all-reduce.9
